TPU v7x, 32 devices: a whole 2x2x4 slice. The times are simulated.
32 devices in a mesh: wide: 8 (over z, y), narrow: 4 (over x, core).
Axes of the slice: x: 2, y: 2, z: 4, core: 2. Of those that a mesh axis runs over, the one named last changes fastest.
Arguments:
- left_edge: bfloat16 [448, 49, 448], P('wide', None, 'narrow'), may hold values from -40 to 40
- corner: bfloat16 [448, 448], P('narrow'), may hold values from -0.25 to 0.25
- right_edge: bfloat16 [448, 49, 448], P('wide', None, 'narrow'), may hold values from -0.25 to 0.25
- single_layer: bfloat16 [2, 2401], replicated, may hold values from -0.71875 to 0.71875
- warm_basis: bfloat16 [49, 448, 448], P(None, 'narrow', 'wide'), may hold values from -0.0390625 to 0.0390625
Outputs:
- new_basis: float32 [448, 49, 448], P('wide', None, 'narrow')
- r_factor: float32 [448, 448], replicated
All inputs are finite; a program needn't handle non-finite values.
Results may differ from a plain program's by a relative error of at most 0.014.
Values may be sent and summed in bfloat16 or wider, within the bound.
No kernel may reach another device: no remote copies, remote signals or barrier semaphores. Data moves between devices by JAX's collectives and lax.ppermute only.
A program may use at most 192 MiB of HBM per device.

v0:
```python
import jax
import jax.numpy as jnp
from jax import lax
from jax.sharding import PartitionSpec as P

BOND = 7


def on_device(left_edge, corner, right_edge, single_layer, warm_basis):
    local_rows = left_edge.shape[0]
    square = left_edge.shape[1]
    breadth = corner.shape[1]
    local_cols = right_edge.shape[2]
    partial_value = jnp.dot(
        left_edge.reshape(local_rows * square, left_edge.shape[2]),
        corner,
        preferred_element_type=jnp.float32,
    )
    half_left = lax.psum(partial_value, "narrow").astype(jnp.bfloat16)
    layer = single_layer.astype(jnp.float32).reshape(single_layer.shape[0], BOND, BOND, BOND, BOND)
    piece = lax.all_gather(right_edge, "wide", axis=0, tiled=True)
    strip_sum = jnp.dot(
        half_left,
        piece.reshape(piece.shape[0], square * local_cols),
        preferred_element_type=jnp.float32,
    )
    strip = (
        strip_sum.astype(jnp.bfloat16)
        .astype(jnp.float32)
        .reshape(local_rows, BOND, BOND, BOND, BOND, local_cols)
    )
    ket_layer = jnp.einsum("iuvlmj,suldr->ivmsdrj", strip, layer)
    enlarged = jnp.einsum("ivmsdrj,svmew->iderwj", ket_layer, layer)
    enlarged = enlarged.astype(jnp.bfloat16).reshape(local_rows * square, square * local_cols)
    piece = lax.all_gather(warm_basis, "wide", axis=2, tiled=True)
    partial_rows = jnp.dot(
        enlarged,
        piece.reshape(square * local_cols, piece.shape[2]),
        preferred_element_type=jnp.float32,
    )
    projected = lax.psum(partial_rows.astype(jnp.bfloat16), "narrow").astype(jnp.float32)
    all_rows = breadth * square
    own_index = lax.axis_index("narrow")
    gram_term = (
        jnp.dot(
            projected.T,
            projected,
            precision=lax.Precision.HIGHEST,
            preferred_element_type=jnp.float32,
        )
        / all_rows
    )
    gram = lax.psum(gram_term, "wide")
    lower = jnp.linalg.cholesky(gram)
    solved = lax.linalg.triangular_solve(lower, projected.T, left_side=True, lower=True)
    own_solved = lax.dynamic_slice_in_dim(solved, own_index * local_cols, local_cols, 0)
    new_basis = own_solved.T.reshape(local_rows, square, local_cols)
    return (new_basis, lower.T)


def solution(mesh):
    placed = (
        P("wide", None, "narrow"),
        P("narrow", None),
        P("wide", None, "narrow"),
        P(),
        P(None, "narrow", "wide"),
    )
    return jax.shard_map(
        on_device,
        mesh=mesh,
        in_specs=placed,
        out_specs=(P("wide", None, "narrow"), P()),
        check_vma=False,
    )
```

profile of v0, /device:TPU:0, one launch (start us, length us, event | category | flops | bytes accessed | tf_op | source)
XLA Modules:
  0.0 761.6 jit_solution(3121338594406813243)
XLA Ops:
  12.1 3.4 fusion.53
  15.5 103.2 %all-reduce.10 = bf16[2744,448]{1,0:T(8,128)(2,1)S(1)} all-reduce(f32[2744,448]{1,0:T(8,128)} %fusion.53), channel_id=1, replica_groups=mesh['wide'=8,'narrow'=4] {'narrow'}, use_global_device_ids=true, to_apply=%region_0.0 | all-reduce | flops 1229312 | bytes 7375872 | tf_op jit(solution)/shard_map/psum | solution.py:19
  118.7 8.6 %copy.14 = bf16[448,49,112]{0,2,1:T(8,128)(2,1)} copy(bf16[448,49,112]{2,0,1:T(8,128)(2,1)} %all-gather.3.cloned.1.call-done) | data formatting | bytes 9834496 | tf_op jit(solution)/shard_map/all_gather | solution.py:21
  127.3 22.5 %convolution_convert_fusion = bf16[2744,5488]{1,0:T(8,128)(2,1)} fusion(bf16[448,5488]{0,1:T(8,128)(2,1)} %bitcast.86, bf16[2744,448]{1,0:T(8,128)(2,1)S(1)} %all-reduce.10), kind=kOutput, calls=%fused_computation.9 | convolution fusion | flops 13507987456 | bytes 37494016 | tf_op jit(solution)/shard_map/dot_general | solution.py:22
  149.8 68.2 %reshape.88 = bf16[56,7,7,7,7,112,1,1]{5,4,3,2,1,0,6,7:T(8,128)(2,1)} reshape(bf16[2744,5488]{1,0:T(8,128)(2,1)} %convolution_convert_fusion) | data formatting | bytes 60236288 | tf_op jit(solution)/shard_map/reshape | solution.py:30
  218.0 42.5 %fusion.4 = bf16[56,7,7,112,2,7,7,1]{3,6,7,5,4,2,1,0:T(8,128)(2,1)} fusion(bf16[56,7,7,7,7,112,1,1]{5,4,3,2,1,0,6,7:T(8,128)(2,1)} %reshape.88, bf16[2,7,7,7,7,1,1,1]{4,3,2,1,0,5,6,7:T(8,128)(2,1)S(1)} %reshape.89), kind=kOutput, calls=%fused_computation.7 | convolution fusion | flops 2951578112 | bytes 90364032 | tf_op jit(solution)/shard_map/iuvlmj,suldr->ivmsdrj/dot_general | solution.py:32
  260.6 64.9 %fusion.3 = bf16[56,7,7,7,7,112]{5,4,2,3,1,0:T(8,128)(2,1)} fusion(bf16[56,7,7,112,2,7,7,1]{3,6,7,5,4,2,1,0:T(8,128)(2,1)} %fusion.4, bf16[2,7,7,7,7,1,1,1]{4,3,2,1,0,7,6,5:T(8,128)(2,1)S(1)} %bitcast.89), kind=kOutput, calls=%fused_computation.6 | convolution fusion | flops 2951578112 | bytes 90364032 | tf_op jit(solution)/shard_map/ivmsdrj,svmew->iderwj/dot_general | solution.py:33
  325.5 25.9 %copy.16 = bf16[56,7,7,7,7,112]{5,4,3,2,1,0:T(8,128)(2,1)} copy(bf16[56,7,7,7,7,112]{5,4,2,3,1,0:T(8,128)(2,1)} %fusion.3) | data formatting | bytes 60236288 | tf_op jit(solution)/shard_map/convert_element_type | solution.py:34
  351.4 55.3 %reshape.66 = bf16[2744,5488]{1,0:T(8,128)(2,1)} reshape(bf16[56,7,7,7,7,112]{5,4,3,2,1,0:T(8,128)(2,1)} %copy.16) | data formatting | bytes 60236288 | tf_op jit(solution)/shard_map/reshape | solution.py:34
  406.7 8.5 %copy.17 = bf16[49,112,448]{2,1,0:T(8,128)(2,1)} copy(bf16[49,112,448]{1,2,0:T(8,128)(2,1)} %all-gather.5.cloned.1.call-done) | data formatting | bytes 9834496 | tf_op jit(solution)/shard_map/all_gather | solution.py:35
  415.3 22.7 %convolution_convert_fusion.1 = bf16[2744,448]{0,1:T(8,128)(2,1)} fusion(bf16[2744,5488]{1,0:T(8,128)(2,1)} %reshape.66, bf16[5488,448]{1,0:T(8,128)(2,1)} %bitcast.87), kind=kOutput, calls=%fused_computation.14 | convolution fusion | flops 13494157312 | bytes 37494016 | tf_op jit(solution)/shard_map/dot_general | solution.py:36
  439.1 57.9 %all-reduce.7.cloned.1.call-done = bf16[2744,448]{0,1:T(8,128)(2,1)} async-done(((bf16[2744,448]{0,1:T(8,128)(2,1)}), bf16[2744,448]{0,1:T(8,128)(2,1)}) %all-reduce.7.cloned.1.call-update) | async-done | bytes 2458640 | tf_op jit(solution)/shard_map/psum | solution.py:41
  497.1 5.0 convolution_multiply_fusion
  502.1 2.6 bitcast_convert_fusion.1
  504.7 74.6 %all-reduce.9.cloned.1.call-done = f32[448,448]{0,1:T(8,128)} async-done(((f32[448,448]{0,1:T(8,128)}), f32[448,448]{0,1:T(8,128)}) %all-reduce.9.cloned.1.call-update) | async-done | bytes 802832 | tf_op jit(solution)/shard_map/psum | solution.py:53
  583.1 11.7 %cholesky.105 = f32[128,128]{1,0:T(8,128)S(1)} custom-call(f32[128,128]{1,0:T(8,128)S(1)} %cholesky.272), custom_call_target="Cholesky" | custom-call | tf_op jit(solution)/shard_map/jit(cholesky)/cholesky | solution.py:54
  594.8 10.4 %custom-call.30 = f32[1,128,128]{1,2,0:T(8,128)} custom-call(f32[1,128,128]{2,1,0:T(8,128)S(1)} %get-tuple-element.33), custom_call_target="InvertDiagBlocksLowerTriangular" | custom-call | tf_op jit(solution)/shard_map/jit(cholesky)/cholesky | solution.py:54
  609.1 12.5 %cholesky.219 = f32[128,128]{1,0:T(8,128)S(1)} custom-call(f32[128,128]{1,0:T(8,128)} %cholesky.276), custom_call_target="Cholesky" | custom-call | tf_op jit(solution)/shard_map/jit(cholesky)/cholesky | solution.py:54
  622.5 10.6 %custom-call.31 = f32[1,128,128]{1,2,0:T(8,128)S(1)} custom-call(f32[1,128,128]{2,1,0:T(8,128)} %get-tuple-element.30), custom_call_target="InvertDiagBlocksLowerTriangular" | custom-call | tf_op jit(solution)/shard_map/jit(cholesky)/cholesky | solution.py:54
  636.1 13.2 %cholesky.240 = f32[128,128]{1,0:T(8,128)} custom-call(f32[128,128]{1,0:T(8,128)} %cholesky.281), custom_call_target="Cholesky" | custom-call | tf_op jit(solution)/shard_map/jit(cholesky)/cholesky | solution.py:54
  651.4 11.3 %custom-call.32 = f32[1,128,128]{1,2,0:T(8,128)} custom-call(f32[1,128,128]{2,1,0:T(8,128)} %get-tuple-element.27), custom_call_target="InvertDiagBlocksLowerTriangular" | custom-call | tf_op jit(solution)/shard_map/jit(cholesky)/cholesky | solution.py:54
  664.8 6.5 cholesky.260
  678.1 10.6 %while.1 = (s32[]{:T(128)}, f32[448,448]{1,0:T(8,128)}, s32[3,2]{0,1:T(2,128)S(1)}, f32[3,128,128]{2,1,0:T(8,128)}, s32[]{:T(128)}) while((s32[]{:T(128)}, f32[448,448]{1,0:T(8,128)}, s32[3,2]{0,1:T(2,128)S(1)}, f32[3,128,128]{2,1,0:T(8,128)}, s32[]{:T(128)}) %tuple.45), condition=%wide.while_cond, body=%wide.while_body.sunk | while | flops 2 | bytes 132705 | solution.py:55
  678.8 2.9 bitcast_dynamic-update-slice_fusion.2
  682.3 2.9 bitcast_dynamic-update-slice_fusion.2
  685.8 2.9 bitcast_dynamic-update-slice_fusion.2
  689.8 39.5 %custom-call.33 = f32[4,128,128]{1,2,0:T(8,128)S(1)} custom-call(f32[4,128,128]{2,1,0:T(8,128)S(1)} %pad_maximum_fusion), custom_call_target="InvertDiagBlocksLowerTriangular" | custom-call | tf_op jit(solution)/shard_map/triangular_solve | solution.py:55
  730.6 2.8 convolution_subtract_fusion.1
  733.4 2.5 fusion.42
  735.9 4.1 convolution_subtract_fusion
  740.0 2.5 fusion.40
  742.5 5.4 fusion.14
  (70 shorter events, 36.9 us)
Async XLA Ops:
  7.2 4.9 copy-start
  7.2 111.5 %all-gather.3.cloned.1.call-start = ((), (), s32[]{:S(2)}) async-start(), calls=%async_computation | async-start | bytes 6322176 | tf_op jit(solution)/shard_map/all_gather | solution.py:21
  7.9 398.8 %all-gather.5.cloned.1.call-start = ((), (), s32[]{:S(2)}) async-start(), calls=%async_computation.1 | async-start | bytes 6322176 | tf_op jit(solution)/shard_map/all_gather | solution.py:35
  8.7 488.4 %all-reduce.7.cloned.1.call-start = ((), (), s32[]{:S(2)}) async-start(), calls=%async_computation.2 | async-start | bytes 5046272 | tf_op jit(solution)/shard_map/psum | solution.py:41
  438.0 141.3 %all-reduce.9.cloned.1.call-start = ((), (), s32[]{:S(2)}) async-start(), calls=%async_computation.3 | async-start | bytes 1835008 | tf_op jit(solution)/shard_map/psum | solution.py:53
  497.1 5.1 copy-start.2
  582.1 0.9 copy-start.5
  607.8 0.7 copy-start.6
  663.7 25.0 %copy-start.7 = (f32[128,64]{1,0:T(8,128)S(1)}, f32[128,64]{1,0:T(8,128)}, u32[]{:S(2)}) copy-start(f32[128,64]{1,0:T(8,128)} %pad_convert_fusion) | copy-start | bytes 98308
  677.2 0.9 copy-start.4
  751.9 2.7 copy-start.1
  752.0 1.4 copy-start.3
Sparse Core Ops, SparseCore 0:
  10.1 92.7 all-gather.2
  105.0 88.7 all-gather.4
  438.1 58.9 all-reduce.6
  502.2 76.9 all-reduce.8
where the time goes:
time: 774 us; the launch traced here: 762 us
  local copies, waits for them, and re-layouts  189 us (24%)
  matrix products  189 us (24%)
  waiting for transfers between devices  134 us (17%)
  other arithmetic  129 us (17%)
  blocking collectives  103 us (13%)
  between operations  17.1 us (2%)
    psum x1, blocking collectives, on_device(): half_left = lax.psum(partial_value, 'narrow').astype(jnp.bfloat16)  103 us
    another operation x14, other arithmetic, on_device(): lower = jnp.linalg.cholesky(gram)  81.4 us
    psum x1, waiting for transfers between devices, on_device(): gram = lax.psum(gram_term, 'wide')  74.6 us
    reshape x1, local copies, waits for them, and re-layouts, on_device(): strip = strip_sum.astype(jnp.bfloat16).astype(jnp.float32).reshape(local_...  68.2 us
    dot_general x1, matrix products, on_device(): enlarged = jnp.einsum('ivmsdrj,svmew->iderwj', ket_layer, layer)  64.9 us
    psum x1, waiting for transfers between devices, on_device(): lax.psum(partial_rows.astype(jnp.bfloat16), 'narrow').astype(jnp.float32)  57.9 us
    reshape x1, local copies, waits for them, and re-layouts, on_device(): enlarged.astype(jnp.bfloat16)  55.3 us
    dot_general x1, matrix products, on_device(): ket_layer = jnp.einsum('iuvlmj,suldr->ivmsdrj', strip, layer)  42.5 us
  transfers between devices with their start and end apart: 4, of which 2 were waited for; matrix products, arithmetic and copies ran while one was open for 39% of the time, Pallas kernels for 0%

commit v1 on v0

--- a/solution.py
+++ b/solution.py
@@ -16,7 +16,7 @@
         corner,
         preferred_element_type=jnp.float32,
     )
-    half_left = lax.psum(partial_value, "narrow").astype(jnp.bfloat16)
+    half_left = jnp.sum(lax.all_gather(partial_value, "narrow"), axis=0).astype(jnp.bfloat16)
     layer = single_layer.astype(jnp.float32).reshape(single_layer.shape[0], BOND, BOND, BOND, BOND)
     piece = lax.all_gather(right_edge, "wide", axis=0, tiled=True)
     strip_sum = jnp.dot(

time: 774 us -> 968 us (1.25)
  waiting for transfers between devices: 134 us -> 423 us
  blocking collectives: 103 us -> 0 us
    all_gather x0 -> x1, waiting for transfers between devices: none -> 119 us  [on_device(): lax.all_gather(partial_value, 'narrow')]
    psum x1 -> x0, blocking collectives: 103 us -> none  [on_device(): half_left = lax.psum(partial_value, 'narrow').astype(jnp.bfloat16)]
    all_gather x1, waiting for transfers between devices: 0.02 us -> 88.7 us  [on_device(): piece = lax.all_gather(right_edge, 'wide', axis=0, tiled=True)]
    all_gather x1, waiting for transfers between devices: 0.01 us -> 82.3 us  [on_device(): piece = lax.all_gather(warm_basis, 'wide', axis=2, tiled=True)]
  transfers between devices with their start and end apart: 4 -> 5, of which waited for: 2 -> 5; matrix products, arithmetic and copies ran while one was open for 39% -> 3% of each run, Pallas kernels for 0% -> 0%
where the time goes in v1:
time: 968 us; the launch traced here: 955 us
  waiting for transfers between devices  423 us (44%)
  matrix products  189 us (20%)
  local copies, waits for them, and re-layouts  187 us (19%)
  other arithmetic  138 us (14%)
  between operations  17 us (2%)
    all_gather x1, waiting for transfers between devices, on_device(): lax.all_gather(partial_value, 'narrow')  119 us
    all_gather x1, waiting for transfers between devices, on_device(): piece = lax.all_gather(right_edge, 'wide', axis=0, tiled=True)  88.7 us
    all_gather x1, waiting for transfers between devices, on_device(): piece = lax.all_gather(warm_basis, 'wide', axis=2, tiled=True)  82.3 us
    another operation x14, other arithmetic, on_device(): lower = jnp.linalg.cholesky(gram)  82.1 us
    psum x1, waiting for transfers between devices, on_device(): gram = lax.psum(gram_term, 'wide')  74.5 us
    reshape x1, local copies, waits for them, and re-layouts, on_device(): strip = strip_sum.astype(jnp.bfloat16).astype(jnp.float32).reshape(local_...  68.2 us
    dot_general x1, matrix products, on_device(): enlarged = jnp.einsum('ivmsdrj,svmew->iderwj', ket_layer, layer)  64.9 us
    psum x1, waiting for transfers between devices, on_device(): lax.psum(partial_rows.astype(jnp.bfloat16), 'narrow').astype(jnp.float32)  57.3 us
  transfers between devices with their start and end apart: 5, of which 5 were waited for; matrix products, arithmetic and copies ran while one was open for 3% of the time, Pallas kernels for 0%

profile of v1, /device:TPU:0, one launch (start us, length us, event | category | flops | bytes accessed | tf_op | source)
XLA Modules:
  0.0 954.7 jit_solution(7898684140776945155)
XLA Ops:
  10.2 3.1 convolution_bitcast_fusion.1
  14.2 88.7 %all-gather.6.cloned.1.call-done = bf16[448,49,112]{2,0,1:T(8,128)(2,1)} async-done(((bf16[56,49,112]{2,0,1:T(8,128)(2,1)}), bf16[448,49,112]{2,0,1:T(8,128)(2,1)}) %all-gather.6.cloned.1.call-update) | async-done | bytes 4917264 | tf_op jit(solution)/shard_map/all_gather | solution.py:21
  102.9 8.6 copy.24
  111.4 82.3 %all-gather.8.cloned.1.call-done = bf16[49,112,448]{1,2,0:T(8,128)(2,1)} async-done(((bf16[49,112,56]{1,2,0:T(8,128)(2,1)}), bf16[49,112,448]{1,2,0:T(8,128)(2,1)}) %all-gather.8.cloned.1.call-update) | async-done | bytes 4917264 | tf_op jit(solution)/shard_map/all_gather | solution.py:35
  193.8 8.6 copy.30
  202.4 118.9 %all-gather.10.cloned.1.call-done = f32[4,2744,448]{1,2,0:T(8,128)} async-done(((f32[1,2744,448]{1,2,0:T(8,128)}), f32[4,2744,448]{1,2,0:T(8,128)}) %all-gather.10.cloned.1.call-update) | async-done | bytes 19669008 | tf_op jit(solution)/shard_map/all_gather | solution.py:19
  321.3 8.0 reduce_sum.9
  329.3 22.6 %convolution_convert_fusion = bf16[2744,5488]{1,0:T(8,128)(2,1)} fusion(bf16[448,5488]{0,1:T(8,128)(2,1)} %bitcast.88, bf16[2744,448]{0,1:T(8,128)(2,1)S(1)} %reduce_sum.9), kind=kOutput, calls=%fused_computation.8 | convolution fusion | flops 13507987456 | bytes 37494016 | tf_op jit(solution)/shard_map/dot_general | solution.py:22
  351.9 68.2 %reshape.64 = bf16[56,7,7,7,7,112]{5,4,3,2,1,0:T(8,128)(2,1)} reshape(bf16[2744,5488]{1,0:T(8,128)(2,1)} %convolution_convert_fusion) | data formatting | bytes 60236288 | tf_op jit(solution)/shard_map/reshape | solution.py:30
  420.1 42.5 %convolution_bitcast_fusion = bf16[56,7,7,2,7,7,112,1]{6,5,4,3,2,1,0,7:T(8,128)(2,1)} fusion(bf16[56,7,7,7,7,112,1,1]{5,4,3,2,1,0,7,6:T(8,128)(2,1)} %bitcast.86, bf16[2,7,7,7,7,1,1,1]{4,3,2,1,0,7,6,5:T(8,128)(2,1)S(1)} %bitcast.90), kind=kOutput, calls=%fused_computation.5 | convolution fusion | flops 2951578112 | bytes 90364032 | tf_op jit(solution)/shard_map/iuvlmj,suldr->ivmsdrj/dot_general | solution.py:32
  462.7 64.9 %fusion.2 = bf16[56,7,7,7,7,112]{5,4,2,3,1,0:T(8,128)(2,1)} fusion(bf16[56,7,7,2,7,7,112,1]{6,5,4,3,2,1,0,7:T(8,128)(2,1)} %convolution_bitcast_fusion, bf16[2,7,7,7,7,1,1,1]{4,3,2,1,0,7,6,5:T(8,128)(2,1)S(1)} %bitcast.91), kind=kOutput, calls=%fused_computation.6 | convolution fusion | flops 2951578112 | bytes 90364032 | tf_op jit(solution)/shard_map/ivmsdrj,svmew->iderwj/dot_general | solution.py:33
  527.6 26.0 %copy.29 = bf16[56,7,7,7,7,112]{5,4,3,2,1,0:T(8,128)(2,1)} copy(bf16[56,7,7,7,7,112]{5,4,2,3,1,0:T(8,128)(2,1)} %fusion.2) | data formatting | bytes 60236288 | tf_op jit(solution)/shard_map/convert_element_type | solution.py:34
  553.5 55.3 %reshape.66 = bf16[2744,5488]{1,0:T(8,128)(2,1)} reshape(bf16[56,7,7,7,7,112]{5,4,3,2,1,0:T(8,128)(2,1)} %copy.29) | data formatting | bytes 60236288 | tf_op jit(solution)/shard_map/reshape | solution.py:34
  608.8 22.6 %convolution_convert_fusion.1 = bf16[2744,448]{0,1:T(8,128)(2,1)} fusion(bf16[2744,5488]{1,0:T(8,128)(2,1)} %reshape.66, bf16[5488,448]{1,0:T(8,128)(2,1)} %bitcast.87), kind=kOutput, calls=%fused_computation.14 | convolution fusion | flops 13494157312 | bytes 37494016 | tf_op jit(solution)/shard_map/dot_general | solution.py:36
  632.6 57.3 %all-reduce.6.cloned.1.call-done = bf16[2744,448]{0,1:T(8,128)(2,1)} async-done(((bf16[2744,448]{0,1:T(8,128)(2,1)}), bf16[2744,448]{0,1:T(8,128)(2,1)}) %all-reduce.6.cloned.1.call-update) | async-done | bytes 2458640 | tf_op jit(solution)/shard_map/psum | solution.py:41
  690.0 5.0 convolution_multiply_fusion
  697.6 74.5 %all-reduce.8.cloned.1.call-done = f32[448,448]{0,1:T(8,128)} async-done(((f32[448,448]{0,1:T(8,128)}), f32[448,448]{0,1:T(8,128)}) %all-reduce.8.cloned.1.call-update) | async-done | bytes 802832 | tf_op jit(solution)/shard_map/psum | solution.py:53
  775.9 11.7 %cholesky.105 = f32[128,128]{1,0:T(8,128)S(1)} custom-call(f32[128,128]{1,0:T(8,128)S(1)} %cholesky.272), custom_call_target="Cholesky" | custom-call | tf_op jit(solution)/shard_map/jit(cholesky)/cholesky | solution.py:54
  788.4 10.6 %custom-call.30 = f32[1,128,128]{1,2,0:T(8,128)S(1)} custom-call(f32[1,128,128]{2,1,0:T(8,128)} %get-tuple-element.35), custom_call_target="InvertDiagBlocksLowerTriangular" | custom-call | tf_op jit(solution)/shard_map/jit(cholesky)/cholesky | solution.py:54
  802.8 12.5 %cholesky.219 = f32[128,128]{1,0:T(8,128)S(1)} custom-call(f32[128,128]{1,0:T(8,128)} %cholesky.276), custom_call_target="Cholesky" | custom-call | tf_op jit(solution)/shard_map/jit(cholesky)/cholesky | solution.py:54
  816.1 10.6 %custom-call.31 = f32[1,128,128]{1,2,0:T(8,128)S(1)} custom-call(f32[1,128,128]{2,1,0:T(8,128)} %get-tuple-element.32), custom_call_target="InvertDiagBlocksLowerTriangular" | custom-call | tf_op jit(solution)/shard_map/jit(cholesky)/cholesky | solution.py:54
  829.8 13.2 %cholesky.240 = f32[128,128]{1,0:T(8,128)} custom-call(f32[128,128]{1,0:T(8,128)} %cholesky.281), custom_call_target="Cholesky" | custom-call | tf_op jit(solution)/shard_map/jit(cholesky)/cholesky | solution.py:54
  845.1 11.3 %custom-call.32 = f32[1,128,128]{1,2,0:T(8,128)} custom-call(f32[1,128,128]{2,1,0:T(8,128)} %get-tuple-element.29), custom_call_target="InvertDiagBlocksLowerTriangular" | custom-call | tf_op jit(solution)/shard_map/jit(cholesky)/cholesky | solution.py:54
  858.5 6.5 cholesky.260
  871.5 10.3 %while.1 = (s32[]{:T(128)}, f32[448,448]{1,0:T(8,128)}, s32[3,2]{0,1:T(2,128)S(1)}, f32[3,128,128]{2,1,0:T(8,128)}, s32[]{:T(128)}) while((s32[]{:T(128)}, f32[448,448]{1,0:T(8,128)}, s32[3,2]{0,1:T(2,128)S(1)}, f32[3,128,128]{2,1,0:T(8,128)}, s32[]{:T(128)}) %tuple.48), condition=%wide.while_cond, body=%wide.while_body.sunk | while | flops 2 | bytes 132705 | solution.py:55
  872.1 2.8 bitcast_dynamic-update-slice_fusion.2
  875.6 2.8 bitcast_dynamic-update-slice_fusion.2
  879.0 2.8 bitcast_dynamic-update-slice_fusion.2
  882.9 39.5 %custom-call.33 = f32[4,128,128]{1,2,0:T(8,128)S(1)} custom-call(f32[4,128,128]{2,1,0:T(8,128)S(1)} %pad_maximum_fusion), custom_call_target="InvertDiagBlocksLowerTriangular" | custom-call | tf_op jit(solution)/shard_map/triangular_solve | solution.py:55
  923.7 2.8 convolution_subtract_fusion.1
  929.0 4.1 convolution_subtract_fusion
  935.7 5.4 fusion.12
  (74 shorter events, 43.8 us)
Async XLA Ops:
  7.2 3.1 copy-start
  7.2 95.7 %all-gather.6.cloned.1.call-start = ((), (), s32[]{:S(2)}) async-start(), calls=%async_computation | async-start | bytes 6322176 | tf_op jit(solution)/shard_map/all_gather | solution.py:21
  7.9 185.9 %all-gather.8.cloned.1.call-start = ((), (), s32[]{:S(2)}) async-start(), calls=%async_computation.1 | async-start | bytes 6322176 | tf_op jit(solution)/shard_map/all_gather | solution.py:35
  8.7 312.7 %all-gather.10.cloned.1.call-start = ((), (), s32[]{:S(2)}) async-start(), calls=%async_computation.4 | async-start | bytes 25231360 | tf_op jit(solution)/shard_map/all_gather | solution.py:19
  13.3 0.7 copy-start.8
  13.3 676.7 %all-reduce.6.cloned.1.call-start = ((), (), s32[]{:S(2)}) async-start(), calls=%async_computation.2 | async-start | bytes 5046272 | tf_op jit(solution)/shard_map/psum | solution.py:41
  631.5 140.6 %all-reduce.8.cloned.1.call-start = ((), (), s32[]{:S(2)}) async-start(), calls=%async_computation.3 | async-start | bytes 1835008 | tf_op jit(solution)/shard_map/psum | solution.py:53
  690.0 5.1 copy-start.2
  775.0 0.9 copy-start.5
  801.5 0.7 copy-start.6
  857.4 24.4 %copy-start.7 = (f32[128,64]{1,0:T(8,128)S(1)}, f32[128,64]{1,0:T(8,128)}, u32[]{:S(2)}) copy-start(f32[128,64]{1,0:T(8,128)} %pad_convert_fusion) | copy-start | bytes 98308
  870.6 0.9 copy-start.4
  945.0 2.7 copy-start.1
  945.2 1.4 copy-start.3
Sparse Core Ops, SparseCore 0:
  10.1 92.7 all-gather.5
  105.0 88.7 all-gather.7
  195.4 125.9 all-gather.9
  631.6 58.2 all-reduce.5
  695.2 76.8 all-reduce.7
